TPU v7x, 128 devices: a whole 4x4x4 slice. The times are simulated.
128 devices in a mesh: mem: 4 (over x), space: 32 (over y, z, core).
Axes of the slice: x: 4, y: 4, z: 4, core: 2. Of those that a mesh axis runs over, the one named last changes fastest.
Arguments:
- log_perm: float32 [8, 128, 128, 128], P('mem', 'space'), may hold values from -4 to 4
- saturation: float32 [128, 128, 128], P('space'), may hold values from 0.1 to 0.9
- pressure_init: float32 [128, 128, 128], P('space'), may hold values from -3 to 3
- wells: int32 [64], replicated, may hold values from 0 to 2097151
- well_rate: float32 [64], replicated, may hold values from -4 to 4
- obs_index: int32 [512, 8], replicated, may hold values from 0 to 2097151, as said below
- obs_weight: float32 [512, 8], replicated, may hold values from -2 to 2
- obs_value: float32 [512], replicated, may hold values from -5 to 5
- obs_var: float32 [512], replicated, may hold values from 0.1 to 1
- noise: float32 [8, 512], replicated, may hold values from -5 to 5
Outputs:
- updated_perm: float32 [8, 128, 128, 128], P(None, 'space', 'mem')
Inputs may be any that keep to these rules, and one draw needn't show every extreme that they name: `obs_index`: observation o reads only cells of the grid row o % 128 along the first dimension.
All inputs are finite; a program needn't handle non-finite values.
Results may differ from a plain program's by a relative error of at most 0.00007.
Values sent between devices are 32-bit elements; how exact they have to be, the bound alone decides.
No kernel may reach another device: no remote copies, remote signals or barrier semaphores. Data moves between devices by JAX's collectives and lax.ppermute only.
A program may use at most 128 MiB of HBM per device.

v0:
```python
import jax
import jax.numpy as jnp
from jax import lax
from jax.sharding import PartitionSpec as P

SWEEPS = 6
water_visc = 1.0
oil_visc = 4.0
time_step = 0.1
storage = 1.0
inflation = 4.0


def padded(cells, sides, width):
    for axis, dim in sides:
        count = lax.axis_size(axis)
        ends = count - 1
        head = lax.slice_in_dim(cells, 0, width, axis=dim)
        tail = lax.slice_in_dim(cells, cells.shape[dim] - width, cells.shape[dim], axis=dim)
        cells = jnp.concatenate(
            [
                lax.ppermute(tail, axis, [(i, (i + 1) % count) for i in range(ends)]),
                cells,
                lax.ppermute(head, axis, [((i + 1) % count, i) for i in range(ends)]),
            ],
            axis=dim,
        )
    return cells


def pad_plane(field):
    return jnp.pad(field, ((0, 0), (0, 0), (1, 1), (1, 1)))


def beside_all(field):
    return [
        field[:, 2:, 1:-1, 1:-1],
        field[:, :-2, 1:-1, 1:-1],
        field[:, 1:-1, 2:, 1:-1],
        field[:, 1:-1, :-2, 1:-1],
        field[:, 1:-1, 1:-1, 2:],
        field[:, 1:-1, 1:-1, :-2],
    ]


def middle(field):
    return field[:, 1:-1, 1:-1, 1:-1]


def props(perm, sat):
    water = sat * sat / water_visc
    oil = (1.0 - sat) * (1.0 - sat) / oil_visc
    total = water + oil
    return (perm * total, water / total)


def saturate(perm_pad, sat_pad, press_pad, source):
    lam, frac = props(perm_pad, sat_pad)
    lam_mid, frac_mid, press_mid = (middle(lam), middle(frac), middle(press_pad))
    outflow = jnp.zeros_like(lam_mid)
    for lam_next, frac_next, press_next in zip(
        beside_all(lam), beside_all(frac), beside_all(press_pad)
    ):
        flux = 0.5 * (lam_mid + lam_next) * (press_mid - press_next)
        outflow = outflow + jnp.maximum(flux, 0.0) * frac_mid + jnp.minimum(flux, 0.0) * frac_next
    water = jnp.maximum(source, 0.0) + jnp.minimum(source, 0.0) * frac_mid
    return jnp.clip(middle(sat_pad) + time_step * (water - outflow), 0.0, 1.0)


def pressure(perm_pad, sat_pad, press_pad, source):
    lam, frac = props(perm_pad, sat_pad)
    lam_mid = middle(lam)
    numer = storage * middle(press_pad) + source
    denom = storage + jnp.zeros_like(lam_mid)
    for lam_next, press_next in zip(beside_all(lam), beside_all(press_pad)):
        trans = 0.5 * (lam_mid + lam_next)
        numer = numer + trans * press_next
        denom = denom + trans
    return numer / denom


def sources(wells, well_rate, first_row, rows, ny, nz):
    plane = ny * nz
    well_x = wells // plane
    rest = wells - well_x * plane
    local_x = well_x - first_row
    valid = (local_x >= 0) & (local_x < rows)
    target = jnp.where(valid, local_x * plane + rest, 0)
    field = jnp.zeros((rows * plane,), jnp.float32).at[target].add(jnp.where(valid, well_rate, 0.0))
    return field.reshape(rows, ny, nz)


def body(
    log_perm,
    saturation,
    pressure_init,
    wells,
    well_rate,
    obs_index,
    obs_weight,
    obs_value,
    obs_var,
    noise,
):
    members, width, ny, nz = log_perm.shape
    shape = (members, width, ny, nz)
    perm = jnp.exp(log_perm)
    sat = jnp.broadcast_to(saturation, shape)
    press = jnp.broadcast_to(pressure_init, shape)
    place = lax.axis_index("space")
    source = sources(wells, well_rate, place * width, width, ny, nz)
    stacked = padded(jnp.stack([perm, sat, press]), (("space", 2),), 1)
    perm_pad = pad_plane(stacked[0])
    sat_ext = stacked[1]
    press_ext = stacked[2]
    for sweep in range(SWEEPS):
        sat = saturate(perm_pad, pad_plane(sat_ext), pad_plane(press_ext), source)
        sat_ext = padded(sat, (("space", 1),), 1)
        press = pressure(perm_pad, pad_plane(sat_ext), pad_plane(press_ext), source)
        if sweep + 1 < SWEEPS:
            press_ext = padded(press, (("space", 1),), 1)
    cells = width * ny * nz
    flat = press.reshape(members, cells)
    local = obs_index - place * cells
    valid = (local >= 0) & (local < cells)
    picked = jnp.take(flat, jnp.where(valid, local, 0), axis=1)
    partial_value = jnp.sum(picked * jnp.where(valid, obs_weight, 0.0)[None], axis=2)
    summed = lax.psum(partial_value, "space")
    predicted = lax.all_gather(summed, "mem", axis=0, tiled=True)
    ensemble = predicted.shape[0]
    high = lax.Precision.HIGHEST
    dev = predicted - jnp.mean(predicted, axis=0, keepdims=True)
    cov = jnp.dot(dev.T, dev, precision=high) / (ensemble - 1) + inflation * jnp.diag(obs_var)
    resid = obs_value[None, :] + jnp.sqrt(inflation * obs_var)[None, :] * noise - predicted
    factor = jnp.linalg.cholesky(cov)
    half = lax.linalg.triangular_solve(factor, resid.T, left_side=True, lower=True)
    solved = lax.linalg.triangular_solve(factor, half, left_side=True, lower=True, transpose_a=True)
    weights = jnp.dot(dev, solved, precision=high) / (ensemble - 1)
    mixing = (
        jnp.eye(ensemble, dtype=jnp.float32) + weights - jnp.mean(weights, axis=0, keepdims=True)
    )
    columns = lax.all_to_all(log_perm, "mem", split_axis=2, concat_axis=0, tiled=True)
    return jnp.tensordot(mixing.T, columns, axes=1, precision=high)


def solution(mesh):
    placed = (
        P("mem", "space", None, None),
        P("space", None, None),
        P("space", None, None),
        P(),
        P(),
        P(),
        P(),
        P(),
        P(),
        P(),
    )
    return jax.shard_map(
        body, mesh=mesh, in_specs=placed, out_specs=P(None, "space", "mem", None), check_vma=False
    )
```

profile of v0, /device:TPU:0, one launch (start us, length us, event | category | flops | bytes accessed | tf_op | source)
XLA Modules:
  0.0 506.8 jit_solution(8930795188840093129)
XLA Ops:
  6.8 3.5 collective-permute-done.1
  15.4 7.9 %collective-permute-start.2 = (f32[2,1,128,128]{3,2,1,0:T(8,128)S(1)}, f32[2,1,128,128]{3,2,1,0:T(8,128)S(1)}, u32[]{:S(2)}, u32[]{:S(2)}) collective-permute-start(f32[2,1,128,128]{3,2,1,0:T(8,128)S(1)} %get-tuple-element.64), channel_id=1, source_target_pairs={{0,1},{1,2},{2,3},{3,4},{4,5},{5,6},{6,7},{7,8},{8,9},{9,10},{10,1... | collective-permute-start | bytes 393224 | tf_op jit(solution)/shard_map/ppermute | solution.py:22
  29.9 5.9 %collective-permute-start.5 = (f32[2,1,128,128]{3,2,1,0:T(8,128)S(1)}, f32[2,1,128,128]{3,2,1,0:T(8,128)S(1)}, u32[]{:S(2)}, u32[]{:S(2)}) collective-permute-start(f32[2,1,128,128]{3,2,1,0:T(8,128)S(1)} %get-tuple-element.63), channel_id=1, source_target_pairs={{0,1},{1,2},{2,3},{3,4},{4,5},{5,6},{6,7},{7,8},{8,9},{9,10},{10,1... | collective-permute-start | bytes 393224 | tf_op jit(solution)/shard_map/ppermute | solution.py:22
  40.0 4.6 collective-permute-start.6
  46.0 3.9 collective-permute-done.7
  53.5 6.3 %collective-permute-start.9 = (f32[2,1,128,128]{3,2,1,0:T(8,128)S(1)}, f32[2,1,128,128]{3,2,1,0:T(8,128)S(1)}, u32[]{:S(2)}, u32[]{:S(2)}) collective-permute-start(f32[2,1,128,128]{3,2,1,0:T(8,128)S(1)} %get-tuple-element.59), channel_id=1, source_target_pairs={{0,1},{1,2},{2,3},{3,4},{4,5},{5,6},{6,7},{7,8},{8,9},{9,10},{10,1... | collective-permute-start | bytes 393224 | tf_op jit(solution)/shard_map/ppermute | solution.py:22
  63.7 4.6 collective-permute-start.10
  69.6 3.9 collective-permute-done.11
  77.1 6.1 %collective-permute-start.13 = (f32[2,1,128,128]{3,2,1,0:T(8,128)S(1)}, f32[2,1,128,128]{3,2,1,0:T(8,128)S(1)}, u32[]{:S(2)}, u32[]{:S(2)}) collective-permute-start(f32[2,1,128,128]{3,2,1,0:T(8,128)S(1)} %get-tuple-element.55), channel_id=1, source_target_pairs={{0,1},{1,2},{2,3},{3,4},{4,5},{5,6},{6,7},{7,8},{8,9},{9,10},{10,1... | collective-permute-start | bytes 393224 | tf_op jit(solution)/shard_map/ppermute | solution.py:22
  88.1 4.6 collective-permute-start.14
  95.2 4.3 all-to-all-start
  100.1 3.3 multiply_divide_fusion.1
  107.7 5.5 %collective-permute-start.17 = (f32[2,1,128,128]{3,2,1,0:T(8,128)}, f32[2,1,128,128]{3,2,1,0:T(8,128)S(1)}, u32[]{:S(2)}, u32[]{:S(2)}) collective-permute-start(f32[2,1,128,128]{3,2,1,0:T(8,128)} %get-tuple-element.51), channel_id=1, source_target_pairs={{0,1},{1,2},{2,3},{3,4},{4,5},{5,6},{6,7},{7,8},{8,9},{9,10},{10,1... | collective-permute-start | bytes 393224 | tf_op jit(solution)/shard_map/ppermute | solution.py:22
  117.5 3.7 fusion.53
  121.2 4.0 collective-permute-start.18
  127.0 6.7 %collective-permute-done.19 = f32[2,1,128,128]{3,2,1,0:T(8,128)S(1)} collective-permute-done((f32[2,1,128,128]{3,2,1,0:T(8,128)S(1)}, f32[2,1,128,128]{3,2,1,0:T(8,128)S(1)}, u32[]{:S(2)}, u32[]{:S(2)}) %collective-permute-start.19) | collective-permute-done | bytes 131104 | tf_op jit(solution)/shard_map/ppermute | solution.py:24
  137.2 7.6 %collective-permute-start.21 = (f32[2,1,128,128]{3,2,1,0:T(8,128)S(1)}, f32[2,1,128,128]{3,2,1,0:T(8,128)S(1)}, u32[]{:S(2)}, u32[]{:S(2)}) collective-permute-start(f32[2,1,128,128]{3,2,1,0:T(8,128)S(1)} %get-tuple-element.47), channel_id=1, source_target_pairs={{0,1},{1,2},{2,3},{3,4},{4,5},{5,6},{6,7},{7,8},{8,9},{9,10},{10,1... | collective-permute-start | bytes 393224 | tf_op jit(solution)/shard_map/ppermute | solution.py:22
  149.9 8.1 %collective-permute-start.22 = (f32[2,1,128,128]{3,2,1,0:T(8,128)}, f32[2,1,128,128]{3,2,1,0:T(8,128)}, u32[]{:S(2)}, u32[]{:S(2)}) collective-permute-start(f32[2,1,128,128]{3,2,1,0:T(8,128)} %get-tuple-element.44), channel_id=1, source_target_pairs={{0,1},{1,2},{2,3},{3,4},{4,5},{5,6},{6,7},{7,8},{8,9},{9,10},{10,1... | collective-permute-start | bytes 393224 | tf_op jit(solution)/shard_map/ppermute | solution.py:22
  167.8 16.7 %copy.27 = f32[2,4,128,128]{0,3,2,1:T(8,128)} copy(f32[2,4,128,128]{3,2,1,0:T(8,128)S(1)} %fusion.35) | data formatting | bytes 1048576 | tf_op jit(solution)/shard_map/div | solution.py:79
  184.5 24.7 %gather_fusion = f32[4096,2]{1,0:T(8,128)} fusion(f32[2,65536]{0,1:T(8,128)} %bitcast.85, s32[4096]{0:T(1024)S(1)} %broadcast_clamp_fusion), kind=kCustom, calls=%fused_computation | custom fusion | bytes 81920 | tf_op jit(solution)/shard_map/jit(_take)/gather | solution.py:126
  209.1 4.3 fusion.1
  213.4 139.6 %psum.7 = f32[2,512]{0,1:T(8,128)S(1)} all-reduce(f32[2,512]{0,1:T(8,128)S(1)} %bitcast.96), channel_id=1, replica_groups=mesh['mem'=4,'space'=32] {'space'}, use_global_device_ids=true, to_apply=%region_2.3 | all-reduce | flops 1024 | bytes 8192 | tf_op jit(solution)/shard_map/psum | solution.py:128
  353.1 12.6 %all-gather = f32[4,2,512]{2,1,0:T(2,128)S(1)} all-gather(f32[1,2,512]{2,1,0:T(2,128)S(1)} %copy.30), channel_id=1, replica_groups=mesh['mem'=4,'space'=32] {'mem'}, dimensions={0}, use_global_device_ids=true | all-gather | bytes 20480 | tf_op jit(solution)/shard_map/all_gather | solution.py:129
  367.4 11.7 %cholesky.103 = f32[128,128]{1,0:T(8,128)S(1)} custom-call(f32[128,128]{1,0:T(8,128)S(1)} %cholesky.263), custom_call_target="Cholesky" | custom-call | tf_op jit(solution)/shard_map/jit(cholesky)/cholesky | solution.py:135
  379.3 9.8 %custom-call.32 = f32[1,128,128]{1,2,0:T(8,128)S(1)} custom-call(f32[1,128,128]{2,1,0:T(8,128)S(1)} %get-tuple-element.77), custom_call_target="InvertDiagBlocksLowerTriangular" | custom-call | tf_op jit(solution)/shard_map/jit(cholesky)/cholesky | solution.py:135
  389.8 11.7 %cholesky.215 = f32[128,128]{1,0:T(8,128)S(1)} custom-call(f32[128,128]{1,0:T(8,128)S(1)} %cholesky.267), custom_call_target="Cholesky" | custom-call | tf_op jit(solution)/shard_map/jit(cholesky)/cholesky | solution.py:135
  401.5 10.0 %custom-call.33 = f32[1,128,128]{1,2,0:T(8,128)S(1)} custom-call(f32[1,128,128]{2,1,0:T(8,128)S(1)} %get-tuple-element.74), custom_call_target="InvertDiagBlocksLowerTriangular" | custom-call | tf_op jit(solution)/shard_map/jit(cholesky)/cholesky | solution.py:135
  412.2 11.7 %cholesky.236 = f32[128,128]{1,0:T(8,128)S(1)} custom-call(f32[128,128]{1,0:T(8,128)S(1)} %cholesky.272), custom_call_target="Cholesky" | custom-call | tf_op jit(solution)/shard_map/jit(cholesky)/cholesky | solution.py:135
  424.6 9.8 %custom-call.34 = f32[1,128,128]{1,2,0:T(8,128)S(1)} custom-call(f32[1,128,128]{2,1,0:T(8,128)S(1)} %get-tuple-element.71), custom_call_target="InvertDiagBlocksLowerTriangular" | custom-call | tf_op jit(solution)/shard_map/jit(cholesky)/cholesky | solution.py:135
  435.0 11.9 %cholesky.253 = f32[128,128]{1,0:T(8,128)S(1)} custom-call(f32[128,128]{1,0:T(8,128)S(1)} %convolution_subtract_fusion.2), custom_call_target="Cholesky" | custom-call | tf_op jit(solution)/shard_map/jit(cholesky)/cholesky | solution.py:135
  451.0 10.5 %while.2 = (s32[]{:T(128)}, f32[512,512]{1,0:T(8,128)S(1)}, s32[4,2]{0,1:T(2,128)S(1)}, f32[4,128,128]{2,1,0:T(8,128)}) while((s32[]{:T(128)}, f32[512,512]{1,0:T(8,128)S(1)}, s32[4,2]{0,1:T(2,128)S(1)}, f32[4,128,128]{2,1,0:T(8,128)}) %tuple.55), condition=%wide.while_cond.clone, body=%wide.while_body.sunk.clone | while | flops 2 | bytes 132697 | solution.py:137
  461.5 40.1 %custom-call.35 = f32[4,128,128]{1,2,0:T(8,128)S(1)} custom-call(f32[4,128,128]{2,1,0:T(8,128)} %get-tuple-element.12), custom_call_target="InvertDiagBlocksLowerTriangular" | custom-call | tf_op jit(solution)/shard_map/triangular_solve | solution.py:137
  (196 shorter events, 93.9 us)
Async XLA Ops:
  3.0 3.8 collective-permute-start
  4.3 6.0 %collective-permute-start.1 = (f32[3,2,1,128,128]{4,3,2,1,0:T(8,128)S(1)}, f32[3,2,1,128,128]{4,3,2,1,0:T(8,128)}, u32[]{:S(2)}, u32[]{:S(2)}) collective-permute-start(f32[3,2,1,128,128]{4,3,2,1,0:T(8,128)S(1)} %get-tuple-element.31), channel_id=1, source_target_pairs={{1,0},{2,1},{3,2},{4,3},{5,4},{6,5},{7,6},{8,7},{9,8},{10,9},{11,1... | collective-permute-start | bytes 1179656 | tf_op jit(solution)/shard_map/ppermute | solution.py:24
  15.4 9.2 %collective-permute-start.2 = (f32[2,1,128,128]{3,2,1,0:T(8,128)S(1)}, f32[2,1,128,128]{3,2,1,0:T(8,128)S(1)}, u32[]{:S(2)}, u32[]{:S(2)}) collective-permute-start(f32[2,1,128,128]{3,2,1,0:T(8,128)S(1)} %get-tuple-element.64), channel_id=1, source_target_pairs={{0,1},{1,2},{2,3},{3,4},{4,5},{5,6},{6,7},{7,8},{8,9},{9,10},{10,1... | collective-permute-start | bytes 393224 | tf_op jit(solution)/shard_map/ppermute | solution.py:22
  23.2 3.2 collective-permute-start.3
  28.6 7.2 %collective-permute-start.4 = (f32[2,1,128,128]{3,2,1,0:T(8,128)S(1)}, f32[2,1,128,128]{3,2,1,0:T(8,128)S(1)}, u32[]{:S(2)}, u32[]{:S(2)}) collective-permute-start(f32[2,1,128,128]{3,2,1,0:T(8,128)S(1)} %get-tuple-element.62), channel_id=1, source_target_pairs={{1,0},{2,1},{3,2},{4,3},{5,4},{6,5},{7,6},{8,7},{9,8},{10,9},{11,1... | collective-permute-start | bytes 393224 | tf_op jit(solution)/shard_map/ppermute | solution.py:24
  29.9 6.8 %collective-permute-start.5 = (f32[2,1,128,128]{3,2,1,0:T(8,128)S(1)}, f32[2,1,128,128]{3,2,1,0:T(8,128)S(1)}, u32[]{:S(2)}, u32[]{:S(2)}) collective-permute-start(f32[2,1,128,128]{3,2,1,0:T(8,128)S(1)} %get-tuple-element.63), channel_id=1, source_target_pairs={{0,1},{1,2},{2,3},{3,4},{4,5},{5,6},{6,7},{7,8},{8,9},{9,10},{10,1... | collective-permute-start | bytes 393224 | tf_op jit(solution)/shard_map/ppermute | solution.py:22
  40.0 5.9 %collective-permute-start.6 = (f32[2,1,128,128]{3,2,1,0:T(8,128)S(1)}, f32[2,1,128,128]{3,2,1,0:T(8,128)S(1)}, u32[]{:S(2)}, u32[]{:S(2)}) collective-permute-start(f32[2,1,128,128]{3,2,1,0:T(8,128)S(1)} %get-tuple-element.60), channel_id=1, source_target_pairs={{0,1},{1,2},{2,3},{3,4},{4,5},{5,6},{6,7},{7,8},{8,9},{9,10},{10,1... | collective-permute-start | bytes 393224 | tf_op jit(solution)/shard_map/ppermute | solution.py:22
  44.7 5.2 %collective-permute-start.7 = (f32[2,1,128,128]{3,2,1,0:T(8,128)S(1)}, f32[2,1,128,128]{3,2,1,0:T(8,128)S(1)}, u32[]{:S(2)}, u32[]{:S(2)}) collective-permute-start(f32[2,1,128,128]{3,2,1,0:T(8,128)S(1)} %get-tuple-element.61), channel_id=1, source_target_pairs={{1,0},{2,1},{3,2},{4,3},{5,4},{6,5},{7,6},{8,7},{9,8},{10,9},{11,1... | collective-permute-start | bytes 393224 | tf_op jit(solution)/shard_map/ppermute | solution.py:24
  52.2 7.6 %collective-permute-start.8 = (f32[2,1,128,128]{3,2,1,0:T(8,128)S(1)}, f32[2,1,128,128]{3,2,1,0:T(8,128)S(1)}, u32[]{:S(2)}, u32[]{:S(2)}) collective-permute-start(f32[2,1,128,128]{3,2,1,0:T(8,128)S(1)} %get-tuple-element.58), channel_id=1, source_target_pairs={{1,0},{2,1},{3,2},{4,3},{5,4},{6,5},{7,6},{8,7},{9,8},{10,9},{11,1... | collective-permute-start | bytes 393224 | tf_op jit(solution)/shard_map/ppermute | solution.py:24
  53.5 7.1 %collective-permute-start.9 = (f32[2,1,128,128]{3,2,1,0:T(8,128)S(1)}, f32[2,1,128,128]{3,2,1,0:T(8,128)S(1)}, u32[]{:S(2)}, u32[]{:S(2)}) collective-permute-start(f32[2,1,128,128]{3,2,1,0:T(8,128)S(1)} %get-tuple-element.59), channel_id=1, source_target_pairs={{0,1},{1,2},{2,3},{3,4},{4,5},{5,6},{6,7},{7,8},{8,9},{9,10},{10,1... | collective-permute-start | bytes 393224 | tf_op jit(solution)/shard_map/ppermute | solution.py:22
  63.7 5.9 %collective-permute-start.10 = (f32[2,1,128,128]{3,2,1,0:T(8,128)S(1)}, f32[2,1,128,128]{3,2,1,0:T(8,128)S(1)}, u32[]{:S(2)}, u32[]{:S(2)}) collective-permute-start(f32[2,1,128,128]{3,2,1,0:T(8,128)S(1)} %get-tuple-element.56), channel_id=1, source_target_pairs={{0,1},{1,2},{2,3},{3,4},{4,5},{5,6},{6,7},{7,8},{8,9},{9,10},{10,1... | collective-permute-start | bytes 393224 | tf_op jit(solution)/shard_map/ppermute | solution.py:22
  68.3 5.2 %collective-permute-start.11 = (f32[2,1,128,128]{3,2,1,0:T(8,128)S(1)}, f32[2,1,128,128]{3,2,1,0:T(8,128)S(1)}, u32[]{:S(2)}, u32[]{:S(2)}) collective-permute-start(f32[2,1,128,128]{3,2,1,0:T(8,128)S(1)} %get-tuple-element.57), channel_id=1, source_target_pairs={{1,0},{2,1},{3,2},{4,3},{5,4},{6,5},{7,6},{8,7},{9,8},{10,9},{11,1... | collective-permute-start | bytes 393224 | tf_op jit(solution)/shard_map/ppermute | solution.py:24
  75.8 7.4 %collective-permute-start.12 = (f32[2,1,128,128]{3,2,1,0:T(8,128)S(1)}, f32[2,1,128,128]{3,2,1,0:T(8,128)S(1)}, u32[]{:S(2)}, u32[]{:S(2)}) collective-permute-start(f32[2,1,128,128]{3,2,1,0:T(8,128)S(1)} %get-tuple-element.54), channel_id=1, source_target_pairs={{1,0},{2,1},{3,2},{4,3},{5,4},{6,5},{7,6},{8,7},{9,8},{10,9},{11,1... | collective-permute-start | bytes 393224 | tf_op jit(solution)/shard_map/ppermute | solution.py:24
  77.1 7.1 %collective-permute-start.13 = (f32[2,1,128,128]{3,2,1,0:T(8,128)S(1)}, f32[2,1,128,128]{3,2,1,0:T(8,128)S(1)}, u32[]{:S(2)}, u32[]{:S(2)}) collective-permute-start(f32[2,1,128,128]{3,2,1,0:T(8,128)S(1)} %get-tuple-element.55), channel_id=1, source_target_pairs={{0,1},{1,2},{2,3},{3,4},{4,5},{5,6},{6,7},{7,8},{8,9},{9,10},{10,1... | collective-permute-start | bytes 393224 | tf_op jit(solution)/shard_map/ppermute | solution.py:22
  88.1 11.3 %collective-permute-start.14 = (f32[2,1,128,128]{3,2,1,0:T(8,128)S(1)}, f32[2,1,128,128]{3,2,1,0:T(8,128)S(1)}, u32[]{:S(2)}, u32[]{:S(2)}) collective-permute-start(f32[2,1,128,128]{3,2,1,0:T(8,128)S(1)} %get-tuple-element.52), channel_id=1, source_target_pairs={{0,1},{1,2},{2,3},{3,4},{4,5},{5,6},{6,7},{7,8},{8,9},{9,10},{10,1... | collective-permute-start | bytes 393224 | tf_op jit(solution)/shard_map/ppermute | solution.py:22
  92.7 7.4 %collective-permute-start.15 = (f32[2,1,128,128]{3,2,1,0:T(8,128)S(1)}, f32[2,1,128,128]{3,2,1,0:T(8,128)}, u32[]{:S(2)}, u32[]{:S(2)}) collective-permute-start(f32[2,1,128,128]{3,2,1,0:T(8,128)S(1)} %get-tuple-element.53), channel_id=1, source_target_pairs={{1,0},{2,1},{3,2},{4,3},{5,4},{6,5},{7,6},{8,7},{9,8},{10,9},{11,1... | collective-permute-start | bytes 393224 | tf_op jit(solution)/shard_map/ppermute | solution.py:24
  95.2 65.7 %all-to-all-start = ((f32[2,4,128,128]{3,1,0,2:T(4,128)}), f32[2,4,128,128]{3,1,0,2:T(4,128)}, u32[]{:S(2)}, u32[]{:S(2)}) async-start(f32[2,4,128,128]{3,1,0,2:T(4,128)} %copy.32), calls=%async_computation | async-start | bytes 1048576 | tf_op jit(solution)/shard_map/all_to_all | solution.py:142
  106.4 9.4 %collective-permute-start.16 = (f32[2,1,128,128]{3,2,1,0:T(8,128)}, f32[2,1,128,128]{3,2,1,0:T(8,128)S(1)}, u32[]{:S(2)}, u32[]{:S(2)}) collective-permute-start(f32[2,1,128,128]{3,2,1,0:T(8,128)} %get-tuple-element.50), channel_id=1, source_target_pairs={{1,0},{2,1},{3,2},{4,3},{5,4},{6,5},{7,6},{8,7},{9,8},{10,9},{11,1... | collective-permute-start | bytes 393224 | tf_op jit(solution)/shard_map/ppermute | solution.py:24
  107.7 8.1 %collective-permute-start.17 = (f32[2,1,128,128]{3,2,1,0:T(8,128)}, f32[2,1,128,128]{3,2,1,0:T(8,128)S(1)}, u32[]{:S(2)}, u32[]{:S(2)}) collective-permute-start(f32[2,1,128,128]{3,2,1,0:T(8,128)} %get-tuple-element.51), channel_id=1, source_target_pairs={{0,1},{1,2},{2,3},{3,4},{4,5},{5,6},{6,7},{7,8},{8,9},{9,10},{10,1... | collective-permute-start | bytes 393224 | tf_op jit(solution)/shard_map/ppermute | solution.py:22
  121.2 5.7 %collective-permute-start.18 = (f32[2,1,128,128]{3,2,1,0:T(8,128)S(1)}, f32[2,1,128,128]{3,2,1,0:T(8,128)S(1)}, u32[]{:S(2)}, u32[]{:S(2)}) collective-permute-start(f32[2,1,128,128]{3,2,1,0:T(8,128)S(1)} %get-tuple-element.48), channel_id=1, source_target_pairs={{0,1},{1,2},{2,3},{3,4},{4,5},{5,6},{6,7},{7,8},{8,9},{9,10},{10,1... | collective-permute-start | bytes 393224 | tf_op jit(solution)/shard_map/ppermute | solution.py:22
  125.2 8.4 %collective-permute-start.19 = (f32[2,1,128,128]{3,2,1,0:T(8,128)S(1)}, f32[2,1,128,128]{3,2,1,0:T(8,128)S(1)}, u32[]{:S(2)}, u32[]{:S(2)}) collective-permute-start(f32[2,1,128,128]{3,2,1,0:T(8,128)S(1)} %get-tuple-element.49), channel_id=1, source_target_pairs={{1,0},{2,1},{3,2},{4,3},{5,4},{6,5},{7,6},{8,7},{9,8},{10,9},{11,1... | collective-permute-start | bytes 393224 | tf_op jit(solution)/shard_map/ppermute | solution.py:24
  135.9 13.1 %copy-start.3 = (f32[2,4,128,128]{3,2,1,0:T(8,128)}, f32[2,4,128,128]{3,2,1,0:T(8,128)S(1)}, u32[]{:S(2)}) copy-start(f32[2,4,128,128]{3,2,1,0:T(8,128)S(1)} %fusion.69) | copy-start | bytes 1572868
  135.9 8.9 %collective-permute-start.20 = (f32[2,1,128,128]{3,2,1,0:T(8,128)S(1)}, f32[2,1,128,128]{3,2,1,0:T(8,128)S(1)}, u32[]{:S(2)}, u32[]{:S(2)}) collective-permute-start(f32[2,1,128,128]{3,2,1,0:T(8,128)S(1)} %get-tuple-element.46), channel_id=1, source_target_pairs={{1,0},{2,1},{3,2},{4,3},{5,4},{6,5},{7,6},{8,7},{9,8},{10,9},{11,1... | collective-permute-start | bytes 393224 | tf_op jit(solution)/shard_map/ppermute | solution.py:24
  137.2 8.5 %collective-permute-start.21 = (f32[2,1,128,128]{3,2,1,0:T(8,128)S(1)}, f32[2,1,128,128]{3,2,1,0:T(8,128)S(1)}, u32[]{:S(2)}, u32[]{:S(2)}) collective-permute-start(f32[2,1,128,128]{3,2,1,0:T(8,128)S(1)} %get-tuple-element.47), channel_id=1, source_target_pairs={{0,1},{1,2},{2,3},{3,4},{4,5},{5,6},{6,7},{7,8},{8,9},{9,10},{10,1... | collective-permute-start | bytes 393224 | tf_op jit(solution)/shard_map/ppermute | solution.py:22
  146.3 13.0 %copy-start.20 = (pred[512,8]{0,1:T(8,128)(4,1)S(1)}, pred[512,8]{0,1:T(8,128)(4,1)}, u32[]{:S(2)}) copy-start(pred[512,8]{0,1:T(8,128)(4,1)} %get-tuple-element.21) | copy-start | bytes 12292
  149.9 13.1 %collective-permute-start.22 = (f32[2,1,128,128]{3,2,1,0:T(8,128)}, f32[2,1,128,128]{3,2,1,0:T(8,128)}, u32[]{:S(2)}, u32[]{:S(2)}) collective-permute-start(f32[2,1,128,128]{3,2,1,0:T(8,128)} %get-tuple-element.44), channel_id=1, source_target_pairs={{0,1},{1,2},{2,3},{3,4},{4,5},{5,6},{6,7},{7,8},{8,9},{9,10},{10,1... | collective-permute-start | bytes 393224 | tf_op jit(solution)/shard_map/ppermute | solution.py:22
  158.0 6.4 %collective-permute-start.23 = (f32[2,1,128,128]{3,2,1,0:T(8,128)}, f32[2,1,128,128]{3,2,1,0:T(8,128)}, u32[]{:S(2)}, u32[]{:S(2)}) collective-permute-start(f32[2,1,128,128]{3,2,1,0:T(8,128)} %get-tuple-element.45), channel_id=1, source_target_pairs={{1,0},{2,1},{3,2},{4,3},{5,4},{6,5},{7,6},{8,7},{9,8},{10,9},{11,1... | collective-permute-start | bytes 393224 | tf_op jit(solution)/shard_map/ppermute | solution.py:24
  184.4 24.7 %copy-start.13 = (f32[512,8]{1,0:T(8,128)S(1)}, f32[512,8]{1,0:T(8,128)}, u32[]{:S(2)}) copy-start(f32[512,8]{1,0:T(8,128)} %copy.29) | copy-start | bytes 49156
  184.4 24.7 %copy-start.15 = (pred[512,8]{1,0:T(8,128)(4,1)S(1)}, pred[512,8]{1,0:T(8,128)(4,1)}, u32[]{:S(2)}) copy-start(pred[512,8]{1,0:T(8,128)(4,1)} %copy.26) | copy-start | bytes 12292
  434.6 67.1 %copy-start.21 = (f32[8,512]{1,0:T(8,128)S(1)}, f32[8,512]{1,0:T(8,128)}, u32[]{:S(2)}) copy-start(f32[8,512]{1,0:T(8,128)} %param.19) | copy-start | bytes 49156
  434.6 67.1 %copy-start.23 = (f32[512]{0:T(512)S(1)}, f32[512]{0:T(512)}, u32[]{:S(2)}) copy-start(f32[512]{0:T(512)} %param.17) | copy-start | bytes 6148
  451.0 53.9 %copy-start.12 = (f32[2,4,4,32,128]{4,0,2,3,1:T(2,128)S(1)}, f32[2,4,4,32,128]{4,0,2,3,1:T(2,128)}, u32[]{:S(2)}) copy-start(f32[2,4,4,32,128]{4,0,2,3,1:T(2,128)} %copy.33) | copy-start | bytes 1572868
  (18 other events, 82.9 us)
where the time goes:
time: 516 us; the launch traced here: 507 us
  other arithmetic  166 us (32%)
  blocking collectives  152 us (29%)
  starting transfers between devices  86.5 us (17%)
  local copies, waits for them, and re-layouts  66.6 us (13%)
  waiting for transfers between devices  24.8 us (5%)
  matrix products  6.63 us (1%)
    psum x1, blocking collectives, body(): summed = lax.psum(partial_value, 'space')  140 us
    another operation x14, other arithmetic, body(): factor = jnp.linalg.cholesky(cov)  78.8 us
    ppermute x12, starting transfers between devices, padded(): lax.ppermute(tail, axis, [(i, (i + 1) % count) for i in range(ends)])  66.4 us
    another operation x3, other arithmetic, body(): lax.linalg.triangular_solve(factor, half, left_side=True, lower=True, tra...  40.2 us
    gather x1, local copies, waits for them, and re-layouts, body(): picked = jnp.take(flat, jnp.where(valid, local, 0), axis=1)  24.7 us
    ppermute x12, waiting for transfers between devices, padded(): lax.ppermute(head, axis, [((i + 1) % count, i) for i in range(ends)])  21.2 us
    min x6, other arithmetic, saturate(): return jnp.clip(middle(sat_pad) + time_step * (water - outflow), 0.0, 1.0)  16.8 us
    div x1, local copies, waits for them, and re-layouts, pressure(): return numer / denom  16.7 us
  transfers between devices with their start and end apart: 25, of which 10 were waited for; matrix products, arithmetic and copies ran while one was open for 5% of the time, Pallas kernels for 0%

commit v1 on v0

--- a/solution.py
+++ b/solution.py
@@ -1,7 +1,9 @@
+import functools
 import jax
 import jax.numpy as jnp
 from jax import lax
 from jax.sharding import PartitionSpec as P
+from jax.lax import axis_size, ppermute
 
 SWEEPS = 6
 water_visc = 1.0
@@ -9,6 +11,17 @@
 time_step = 0.1
 storage = 1.0
 inflation = 4.0
+
+
+def plan_blocks_in(unit, peer_axis):
+    count_all = axis_size(peer_axis)
+    later = unit
+    for h in [rr for rr in (1, 2, 4, 8, 16) if rr < count_all]:
+        later = later + ppermute(later, peer_axis, tuple(((it, it ^ h) for it in range(count_all))))
+    return later
+
+
+press_tokens = functools.partial(plan_blocks_in, peer_axis="space")
 
 
 def padded(cells, sides, width):
@@ -125,7 +138,7 @@
     valid = (local >= 0) & (local < cells)
     picked = jnp.take(flat, jnp.where(valid, local, 0), axis=1)
     partial_value = jnp.sum(picked * jnp.where(valid, obs_weight, 0.0)[None], axis=2)
-    summed = lax.psum(partial_value, "space")
+    summed = press_tokens(partial_value)
     predicted = lax.all_gather(summed, "mem", axis=0, tiled=True)
     ensemble = predicted.shape[0]
     high = lax.Precision.HIGHEST

time: 516 us -> 434 us (0.84)
  blocking collectives: 152 us -> 12.2 us
  starting transfers between devices: 86.5 us -> 126 us
  waiting for transfers between devices: 24.8 us -> 52.2 us
  local copies, waits for them, and re-layouts: 66.6 us -> 58.6 us
    psum x1 -> x0, blocking collectives: 140 us -> none  [body(): summed = lax.psum(partial_value, 'space')]
    ppermute x0 -> x5, starting transfers between devices: none -> 37.1 us  [plan_blocks_in(): ppermute(later, peer_axis, tuple(((it, it ^ h) for it in range(count_all))))]
    ppermute x0 -> x5, waiting for transfers between devices: none -> 21.1 us  [plan_blocks_in(): ppermute(later, peer_axis, tuple(((it, it ^ h) for it in range(count_all))))]
    ppermute x12, waiting for transfers between devices: 21.2 us -> 27 us  [padded(): lax.ppermute(head, axis, [((i + 1) % count, i) for i in range(ends)])]
  transfers between devices with their start and end apart: 25 -> 30, of which waited for: 10 -> 16; matrix products, arithmetic and copies ran while one was open for 5% -> 1% of each run, Pallas kernels for 0% -> 0%
where the time goes in v1:
time: 434 us; the launch traced here: 425 us
  other arithmetic  165 us (38%)
  starting transfers between devices  126 us (29%)
  local copies, waits for them, and re-layouts  58.6 us (14%)
  waiting for transfers between devices  52.2 us (12%)
  blocking collectives  12.2 us (3%)
  matrix products  6.63 us (2%)
    another operation x14, other arithmetic, body(): factor = jnp.linalg.cholesky(cov)  78.9 us
    ppermute x12, starting transfers between devices, padded(): lax.ppermute(tail, axis, [(i, (i + 1) % count) for i in range(ends)])  68.8 us
    another operation x3, other arithmetic, body(): lax.linalg.triangular_solve(factor, half, left_side=True, lower=True, tra...  39.4 us
    ppermute x5, starting transfers between devices, plan_blocks_in(): ppermute(later, peer_axis, tuple(((it, it ^ h) for it in range(count_all))))  37.1 us
    ppermute x12, waiting for transfers between devices, padded(): lax.ppermute(head, axis, [((i + 1) % count, i) for i in range(ends)])  27 us
    gather x1, local copies, waits for them, and re-layouts, body(): picked = jnp.take(flat, jnp.where(valid, local, 0), axis=1)  21.3 us
    ppermute x5, waiting for transfers between devices, plan_blocks_in(): ppermute(later, peer_axis, tuple(((it, it ^ h) for it in range(count_all))))  21.1 us
    min x6, other arithmetic, saturate(): return jnp.clip(middle(sat_pad) + time_step * (water - outflow), 0.0, 1.0)  18.1 us
  transfers between devices with their start and end apart: 30, of which 16 were waited for; matrix products, arithmetic and copies ran while one was open for 1% of the time, Pallas kernels for 0%

profile of v1, /device:TPU:0, one launch (start us, length us, event | category | flops | bytes accessed | tf_op | source)
XLA Modules:
  0.0 425.4 jit_solution(16498821443412667967)
XLA Ops:
  15.2 7.9 %collective-permute-start.2 = (f32[2,1,128,128]{3,2,1,0:T(8,128)S(1)}, f32[2,1,128,128]{3,2,1,0:T(8,128)S(1)}, u32[]{:S(2)}, u32[]{:S(2)}) collective-permute-start(f32[2,1,128,128]{3,2,1,0:T(8,128)S(1)} %get-tuple-element.64), channel_id=1, source_target_pairs={{0,1},{1,2},{2,3},{3,4},{4,5},{5,6},{6,7},{7,8},{8,9},{9,10},{10,1... | collective-permute-start | bytes 393224 | tf_op jit(solution)/shard_map/ppermute | solution.py:35
  29.8 5.9 %collective-permute-start.5 = (f32[2,1,128,128]{3,2,1,0:T(8,128)S(1)}, f32[2,1,128,128]{3,2,1,0:T(8,128)S(1)}, u32[]{:S(2)}, u32[]{:S(2)}) collective-permute-start(f32[2,1,128,128]{3,2,1,0:T(8,128)S(1)} %get-tuple-element.63), channel_id=1, source_target_pairs={{0,1},{1,2},{2,3},{3,4},{4,5},{5,6},{6,7},{7,8},{8,9},{9,10},{10,1... | collective-permute-start | bytes 393224 | tf_op jit(solution)/shard_map/ppermute | solution.py:35
  39.9 4.6 %collective-permute-start.6 = (f32[2,1,128,128]{3,2,1,0:T(8,128)S(1)}, f32[2,1,128,128]{3,2,1,0:T(8,128)S(1)}, u32[]{:S(2)}, u32[]{:S(2)}) collective-permute-start(f32[2,1,128,128]{3,2,1,0:T(8,128)S(1)} %get-tuple-element.60), channel_id=1, source_target_pairs={{0,1},{1,2},{2,3},{3,4},{4,5},{5,6},{6,7},{7,8},{8,9},{9,10},{10,1... | collective-permute-start | bytes 393224 | tf_op jit(solution)/shard_map/ppermute | solution.py:35
  53.3 6.3 %collective-permute-start.9 = (f32[2,1,128,128]{3,2,1,0:T(8,128)S(1)}, f32[2,1,128,128]{3,2,1,0:T(8,128)S(1)}, u32[]{:S(2)}, u32[]{:S(2)}) collective-permute-start(f32[2,1,128,128]{3,2,1,0:T(8,128)S(1)} %get-tuple-element.59), channel_id=1, source_target_pairs={{0,1},{1,2},{2,3},{3,4},{4,5},{5,6},{6,7},{7,8},{8,9},{9,10},{10,1... | collective-permute-start | bytes 393224 | tf_op jit(solution)/shard_map/ppermute | solution.py:35
  63.5 4.6 %collective-permute-start.10 = (f32[2,1,128,128]{3,2,1,0:T(8,128)S(1)}, f32[2,1,128,128]{3,2,1,0:T(8,128)S(1)}, u32[]{:S(2)}, u32[]{:S(2)}) collective-permute-start(f32[2,1,128,128]{3,2,1,0:T(8,128)S(1)} %get-tuple-element.56), channel_id=1, source_target_pairs={{0,1},{1,2},{2,3},{3,4},{4,5},{5,6},{6,7},{7,8},{8,9},{9,10},{10,1... | collective-permute-start | bytes 393224 | tf_op jit(solution)/shard_map/ppermute | solution.py:35
  76.9 6.1 %collective-permute-start.13 = (f32[2,1,128,128]{3,2,1,0:T(8,128)S(1)}, f32[2,1,128,128]{3,2,1,0:T(8,128)S(1)}, u32[]{:S(2)}, u32[]{:S(2)}) collective-permute-start(f32[2,1,128,128]{3,2,1,0:T(8,128)S(1)} %get-tuple-element.55), channel_id=1, source_target_pairs={{0,1},{1,2},{2,3},{3,4},{4,5},{5,6},{6,7},{7,8},{8,9},{9,10},{10,1... | collective-permute-start | bytes 393224 | tf_op jit(solution)/shard_map/ppermute | solution.py:35
  87.2 4.6 %collective-permute-start.14 = (f32[2,1,128,128]{3,2,1,0:T(8,128)S(1)}, f32[2,1,128,128]{3,2,1,0:T(8,128)S(1)}, u32[]{:S(2)}, u32[]{:S(2)}) collective-permute-start(f32[2,1,128,128]{3,2,1,0:T(8,128)S(1)} %get-tuple-element.52), channel_id=1, source_target_pairs={{0,1},{1,2},{2,3},{3,4},{4,5},{5,6},{6,7},{7,8},{8,9},{9,10},{10,1... | collective-permute-start | bytes 393224 | tf_op jit(solution)/shard_map/ppermute | solution.py:35
  103.3 6.1 %collective-permute-start.17 = (f32[2,1,128,128]{3,2,1,0:T(8,128)}, f32[2,1,128,128]{3,2,1,0:T(8,128)S(1)}, u32[]{:S(2)}, u32[]{:S(2)}) collective-permute-start(f32[2,1,128,128]{3,2,1,0:T(8,128)} %get-tuple-element.51), channel_id=1, source_target_pairs={{0,1},{1,2},{2,3},{3,4},{4,5},{5,6},{6,7},{7,8},{8,9},{9,10},{10,1... | collective-permute-start | bytes 393224 | tf_op jit(solution)/shard_map/ppermute | solution.py:35
  116.8 6.6 %collective-permute-start.18 = (f32[2,1,128,128]{3,2,1,0:T(8,128)S(1)}, f32[2,1,128,128]{3,2,1,0:T(8,128)S(1)}, u32[]{:S(2)}, u32[]{:S(2)}) collective-permute-start(f32[2,1,128,128]{3,2,1,0:T(8,128)S(1)} %get-tuple-element.48), channel_id=1, source_target_pairs={{0,1},{1,2},{2,3},{3,4},{4,5},{5,6},{6,7},{7,8},{8,9},{9,10},{10,1... | collective-permute-start | bytes 393224 | tf_op jit(solution)/shard_map/ppermute | solution.py:35
  138.2 8.3 %collective-permute-start.21 = (f32[2,1,128,128]{3,2,1,0:T(8,128)}, f32[2,1,128,128]{3,2,1,0:T(8,128)S(1)}, u32[]{:S(2)}, u32[]{:S(2)}) collective-permute-start(f32[2,1,128,128]{3,2,1,0:T(8,128)} %get-tuple-element.47), channel_id=1, source_target_pairs={{0,1},{1,2},{2,3},{3,4},{4,5},{5,6},{6,7},{7,8},{8,9},{9,10},{10,1... | collective-permute-start | bytes 393224 | tf_op jit(solution)/shard_map/ppermute | solution.py:35
  153.0 6.6 %collective-permute-start.22 = (f32[2,1,128,128]{3,2,1,0:T(8,128)S(1)}, f32[2,1,128,128]{3,2,1,0:T(8,128)S(1)}, u32[]{:S(2)}, u32[]{:S(2)}) collective-permute-start(f32[2,1,128,128]{3,2,1,0:T(8,128)S(1)} %get-tuple-element.44), channel_id=1, source_target_pairs={{0,1},{1,2},{2,3},{3,4},{4,5},{5,6},{6,7},{7,8},{8,9},{9,10},{10,1... | collective-permute-start | bytes 393224 | tf_op jit(solution)/shard_map/ppermute | solution.py:35
  160.9 6.1 %collective-permute-done.23 = f32[2,1,128,128]{3,2,1,0:T(8,128)S(1)} collective-permute-done((f32[2,1,128,128]{3,2,1,0:T(8,128)S(1)}, f32[2,1,128,128]{3,2,1,0:T(8,128)S(1)}, u32[]{:S(2)}, u32[]{:S(2)}) %collective-permute-start.23) | collective-permute-done | bytes 131104 | tf_op jit(solution)/shard_map/ppermute | solution.py:37
  169.3 16.7 %copy.27 = f32[2,4,128,128]{0,3,2,1:T(8,128)} copy(f32[2,4,128,128]{3,2,1,0:T(8,128)S(1)} %fusion.35) | data formatting | bytes 1048576 | tf_op jit(solution)/shard_map/div | solution.py:92
  186.0 21.3 %gather_fusion = f32[4096,2]{1,0:T(8,128)S(1)} fusion(f32[2,65536]{0,1:T(8,128)} %bitcast.87, s32[4096]{0:T(1024)S(1)} %broadcast_clamp_fusion), kind=kCustom, calls=%fused_computation | custom fusion | bytes 81920 | tf_op jit(solution)/shard_map/jit(_take)/gather | solution.py:139
  210.2 5.6 %collective-permute-start.24 = (f32[2,512]{0,1:T(8,128)S(1)}, f32[2,512]{0,1:T(8,128)S(1)}, u32[]{:S(2)}, u32[]{:S(2)}) collective-permute-start(f32[2,512]{0,1:T(8,128)S(1)} %bitcast.98), channel_id=1, source_target_pairs={{0,1},{1,0},{2,3},{3,2},{4,5},{5,4},{6,7},{7,6},{8,9},{9,8},{10,11... | collective-permute-start | bytes 12296 | tf_op jit(solution)/shard_map/ppermute | solution.py:20
  217.0 4.4 %all-to-all-start = ((f32[2,4,128,128]{3,1,0,2:T(4,128)}), f32[2,4,128,128]{3,1,0,2:T(4,128)S(1)}, u32[]{:S(2)}, u32[]{:S(2)}) async-start(f32[2,4,128,128]{3,1,0,2:T(4,128)} %copy.32), calls=%async_computation | async-start | bytes 1048576 | tf_op jit(solution)/shard_map/all_to_all | solution.py:155
  221.4 9.3 %collective-permute-start.25 = (f32[2,512]{0,1:T(8,128)S(1)}, f32[2,512]{0,1:T(8,128)S(1)}, u32[]{:S(2)}, u32[]{:S(2)}) collective-permute-start(f32[2,512]{0,1:T(8,128)S(1)} %bitcast_add_fusion), channel_id=1, source_target_pairs={{0,2},{1,3},{2,0},{3,1},{4,6},{5,7},{6,4},{7,5},{8,10},{9,11},{10,... | collective-permute-start | bytes 12296 | tf_op jit(solution)/shard_map/ppermute | solution.py:20
  230.7 6.2 %collective-permute-done.25 = f32[2,512]{0,1:T(8,128)S(1)} collective-permute-done((f32[2,512]{0,1:T(8,128)S(1)}, f32[2,512]{0,1:T(8,128)S(1)}, u32[]{:S(2)}, u32[]{:S(2)}) %collective-permute-start.25) | collective-permute-done | bytes 4128 | tf_op jit(solution)/shard_map/ppermute | solution.py:20
  237.0 17.7 %collective-permute-start.26 = (f32[2,512]{0,1:T(8,128)S(1)}, f32[2,512]{0,1:T(8,128)S(1)}, u32[]{:S(2)}, u32[]{:S(2)}) collective-permute-start(f32[2,512]{0,1:T(8,128)S(1)} %add.1001), channel_id=1, source_target_pairs={{0,4},{1,5},{2,6},{3,7},{4,0},{5,1},{6,2},{7,3},{8,12},{9,13},{10,... | collective-permute-start | bytes 12296 | tf_op jit(solution)/shard_map/ppermute | solution.py:20
  254.6 5.6 %collective-permute-done.26 = f32[2,512]{0,1:T(8,128)S(1)} collective-permute-done((f32[2,512]{0,1:T(8,128)S(1)}, f32[2,512]{0,1:T(8,128)S(1)}, u32[]{:S(2)}, u32[]{:S(2)}) %collective-permute-start.26) | collective-permute-done | bytes 4128 | tf_op jit(solution)/shard_map/ppermute | solution.py:20
  262.0 5.2 %collective-permute-done.27 = f32[2,512]{0,1:T(8,128)S(1)} collective-permute-done((f32[2,512]{0,1:T(8,128)S(1)}, f32[2,512]{0,1:T(8,128)S(1)}, u32[]{:S(2)}, u32[]{:S(2)}) %collective-permute-start.27) | collective-permute-done | bytes 4128 | tf_op jit(solution)/shard_map/ppermute | solution.py:20
  271.2 4.0 collective-permute-done.28
  275.3 12.2 %all-gather = f32[4,2,512]{2,1,0:T(2,128)S(1)} all-gather(f32[1,2,512]{2,1,0:T(2,128)S(1)} %copy.30), channel_id=1, replica_groups=mesh['mem'=4,'space'=32] {'mem'}, dimensions={0}, use_global_device_ids=true | all-gather | bytes 20480 | tf_op jit(solution)/shard_map/all_gather | solution.py:142
  289.2 11.7 %cholesky.103 = f32[128,128]{1,0:T(8,128)S(1)} custom-call(f32[128,128]{1,0:T(8,128)S(1)} %cholesky.263), custom_call_target="Cholesky" | custom-call | tf_op jit(solution)/shard_map/jit(cholesky)/cholesky | solution.py:148
  301.1 9.8 %custom-call.32 = f32[1,128,128]{1,2,0:T(8,128)S(1)} custom-call(f32[1,128,128]{2,1,0:T(8,128)S(1)} %get-tuple-element.77), custom_call_target="InvertDiagBlocksLowerTriangular" | custom-call | tf_op jit(solution)/shard_map/jit(cholesky)/cholesky | solution.py:148
  311.6 11.7 %cholesky.215 = f32[128,128]{1,0:T(8,128)S(1)} custom-call(f32[128,128]{1,0:T(8,128)S(1)} %cholesky.267), custom_call_target="Cholesky" | custom-call | tf_op jit(solution)/shard_map/jit(cholesky)/cholesky | solution.py:148
  323.3 10.0 %custom-call.33 = f32[1,128,128]{1,2,0:T(8,128)S(1)} custom-call(f32[1,128,128]{2,1,0:T(8,128)S(1)} %get-tuple-element.74), custom_call_target="InvertDiagBlocksLowerTriangular" | custom-call | tf_op jit(solution)/shard_map/jit(cholesky)/cholesky | solution.py:148
  334.0 11.7 %cholesky.236 = f32[128,128]{1,0:T(8,128)S(1)} custom-call(f32[128,128]{1,0:T(8,128)S(1)} %cholesky.272), custom_call_target="Cholesky" | custom-call | tf_op jit(solution)/shard_map/jit(cholesky)/cholesky | solution.py:148
  346.4 9.8 %custom-call.34 = f32[1,128,128]{1,2,0:T(8,128)S(1)} custom-call(f32[1,128,128]{2,1,0:T(8,128)S(1)} %get-tuple-element.71), custom_call_target="InvertDiagBlocksLowerTriangular" | custom-call | tf_op jit(solution)/shard_map/jit(cholesky)/cholesky | solution.py:148
  356.8 11.9 %cholesky.253 = f32[128,128]{1,0:T(8,128)S(1)} custom-call(f32[128,128]{1,0:T(8,128)S(1)} %convolution_subtract_fusion.2), custom_call_target="Cholesky" | custom-call | tf_op jit(solution)/shard_map/jit(cholesky)/cholesky | solution.py:148
  372.9 8.1 %while.2 = (s32[]{:T(128)}, f32[512,512]{1,0:T(8,128)S(1)}, s32[4,2]{0,1:T(2,128)S(1)}, f32[4,128,128]{2,1,0:T(8,128)S(1)}) while((s32[]{:T(128)}, f32[512,512]{1,0:T(8,128)S(1)}, s32[4,2]{0,1:T(2,128)S(1)}, f32[4,128,128]{2,1,0:T(8,128)S(1)}) %tuple.55), condition=%wide.while_cond.clone, body=%wide.while_body.sunk.clone | while | flops 2 | bytes 131173 | solution.py:150
  380.9 39.3 %custom-call.35 = f32[4,128,128]{1,2,0:T(8,128)S(1)} custom-call(f32[4,128,128]{2,1,0:T(8,128)S(1)} %get-tuple-element.12), custom_call_target="InvertDiagBlocksLowerTriangular" | custom-call | tf_op jit(solution)/shard_map/triangular_solve | solution.py:150
  (208 shorter events, 123.4 us)
Async XLA Ops:
  3.0 3.8 collective-permute-start
  4.3 6.0 %collective-permute-start.1 = (f32[3,2,1,128,128]{4,3,2,1,0:T(8,128)S(1)}, f32[3,2,1,128,128]{4,3,2,1,0:T(8,128)}, u32[]{:S(2)}, u32[]{:S(2)}) collective-permute-start(f32[3,2,1,128,128]{4,3,2,1,0:T(8,128)S(1)} %get-tuple-element.31), channel_id=1, source_target_pairs={{1,0},{2,1},{3,2},{4,3},{5,4},{6,5},{7,6},{8,7},{9,8},{10,9},{11,1... | collective-permute-start | bytes 1179656 | tf_op jit(solution)/shard_map/ppermute | solution.py:37
  15.2 9.2 %collective-permute-start.2 = (f32[2,1,128,128]{3,2,1,0:T(8,128)S(1)}, f32[2,1,128,128]{3,2,1,0:T(8,128)S(1)}, u32[]{:S(2)}, u32[]{:S(2)}) collective-permute-start(f32[2,1,128,128]{3,2,1,0:T(8,128)S(1)} %get-tuple-element.64), channel_id=1, source_target_pairs={{0,1},{1,2},{2,3},{3,4},{4,5},{5,6},{6,7},{7,8},{8,9},{9,10},{10,1... | collective-permute-start | bytes 393224 | tf_op jit(solution)/shard_map/ppermute | solution.py:35
  23.1 3.2 collective-permute-start.3
  28.5 7.2 %collective-permute-start.4 = (f32[2,1,128,128]{3,2,1,0:T(8,128)S(1)}, f32[2,1,128,128]{3,2,1,0:T(8,128)S(1)}, u32[]{:S(2)}, u32[]{:S(2)}) collective-permute-start(f32[2,1,128,128]{3,2,1,0:T(8,128)S(1)} %get-tuple-element.62), channel_id=1, source_target_pairs={{1,0},{2,1},{3,2},{4,3},{5,4},{6,5},{7,6},{8,7},{9,8},{10,9},{11,1... | collective-permute-start | bytes 393224 | tf_op jit(solution)/shard_map/ppermute | solution.py:37
  29.8 6.8 %collective-permute-start.5 = (f32[2,1,128,128]{3,2,1,0:T(8,128)S(1)}, f32[2,1,128,128]{3,2,1,0:T(8,128)S(1)}, u32[]{:S(2)}, u32[]{:S(2)}) collective-permute-start(f32[2,1,128,128]{3,2,1,0:T(8,128)S(1)} %get-tuple-element.63), channel_id=1, source_target_pairs={{0,1},{1,2},{2,3},{3,4},{4,5},{5,6},{6,7},{7,8},{8,9},{9,10},{10,1... | collective-permute-start | bytes 393224 | tf_op jit(solution)/shard_map/ppermute | solution.py:35
  39.9 5.9 %collective-permute-start.6 = (f32[2,1,128,128]{3,2,1,0:T(8,128)S(1)}, f32[2,1,128,128]{3,2,1,0:T(8,128)S(1)}, u32[]{:S(2)}, u32[]{:S(2)}) collective-permute-start(f32[2,1,128,128]{3,2,1,0:T(8,128)S(1)} %get-tuple-element.60), channel_id=1, source_target_pairs={{0,1},{1,2},{2,3},{3,4},{4,5},{5,6},{6,7},{7,8},{8,9},{9,10},{10,1... | collective-permute-start | bytes 393224 | tf_op jit(solution)/shard_map/ppermute | solution.py:35
  44.5 5.2 %collective-permute-start.7 = (f32[2,1,128,128]{3,2,1,0:T(8,128)S(1)}, f32[2,1,128,128]{3,2,1,0:T(8,128)S(1)}, u32[]{:S(2)}, u32[]{:S(2)}) collective-permute-start(f32[2,1,128,128]{3,2,1,0:T(8,128)S(1)} %get-tuple-element.61), channel_id=1, source_target_pairs={{1,0},{2,1},{3,2},{4,3},{5,4},{6,5},{7,6},{8,7},{9,8},{10,9},{11,1... | collective-permute-start | bytes 393224 | tf_op jit(solution)/shard_map/ppermute | solution.py:37
  52.0 7.6 %collective-permute-start.8 = (f32[2,1,128,128]{3,2,1,0:T(8,128)S(1)}, f32[2,1,128,128]{3,2,1,0:T(8,128)S(1)}, u32[]{:S(2)}, u32[]{:S(2)}) collective-permute-start(f32[2,1,128,128]{3,2,1,0:T(8,128)S(1)} %get-tuple-element.58), channel_id=1, source_target_pairs={{1,0},{2,1},{3,2},{4,3},{5,4},{6,5},{7,6},{8,7},{9,8},{10,9},{11,1... | collective-permute-start | bytes 393224 | tf_op jit(solution)/shard_map/ppermute | solution.py:37
  53.3 7.1 %collective-permute-start.9 = (f32[2,1,128,128]{3,2,1,0:T(8,128)S(1)}, f32[2,1,128,128]{3,2,1,0:T(8,128)S(1)}, u32[]{:S(2)}, u32[]{:S(2)}) collective-permute-start(f32[2,1,128,128]{3,2,1,0:T(8,128)S(1)} %get-tuple-element.59), channel_id=1, source_target_pairs={{0,1},{1,2},{2,3},{3,4},{4,5},{5,6},{6,7},{7,8},{8,9},{9,10},{10,1... | collective-permute-start | bytes 393224 | tf_op jit(solution)/shard_map/ppermute | solution.py:35
  63.5 5.9 %collective-permute-start.10 = (f32[2,1,128,128]{3,2,1,0:T(8,128)S(1)}, f32[2,1,128,128]{3,2,1,0:T(8,128)S(1)}, u32[]{:S(2)}, u32[]{:S(2)}) collective-permute-start(f32[2,1,128,128]{3,2,1,0:T(8,128)S(1)} %get-tuple-element.56), channel_id=1, source_target_pairs={{0,1},{1,2},{2,3},{3,4},{4,5},{5,6},{6,7},{7,8},{8,9},{9,10},{10,1... | collective-permute-start | bytes 393224 | tf_op jit(solution)/shard_map/ppermute | solution.py:35
  68.1 5.2 %collective-permute-start.11 = (f32[2,1,128,128]{3,2,1,0:T(8,128)S(1)}, f32[2,1,128,128]{3,2,1,0:T(8,128)S(1)}, u32[]{:S(2)}, u32[]{:S(2)}) collective-permute-start(f32[2,1,128,128]{3,2,1,0:T(8,128)S(1)} %get-tuple-element.57), channel_id=1, source_target_pairs={{1,0},{2,1},{3,2},{4,3},{5,4},{6,5},{7,6},{8,7},{9,8},{10,9},{11,1... | collective-permute-start | bytes 393224 | tf_op jit(solution)/shard_map/ppermute | solution.py:37
  75.6 7.4 %collective-permute-start.12 = (f32[2,1,128,128]{3,2,1,0:T(8,128)S(1)}, f32[2,1,128,128]{3,2,1,0:T(8,128)S(1)}, u32[]{:S(2)}, u32[]{:S(2)}) collective-permute-start(f32[2,1,128,128]{3,2,1,0:T(8,128)S(1)} %get-tuple-element.54), channel_id=1, source_target_pairs={{1,0},{2,1},{3,2},{4,3},{5,4},{6,5},{7,6},{8,7},{9,8},{10,9},{11,1... | collective-permute-start | bytes 393224 | tf_op jit(solution)/shard_map/ppermute | solution.py:37
  76.9 7.1 %collective-permute-start.13 = (f32[2,1,128,128]{3,2,1,0:T(8,128)S(1)}, f32[2,1,128,128]{3,2,1,0:T(8,128)S(1)}, u32[]{:S(2)}, u32[]{:S(2)}) collective-permute-start(f32[2,1,128,128]{3,2,1,0:T(8,128)S(1)} %get-tuple-element.55), channel_id=1, source_target_pairs={{0,1},{1,2},{2,3},{3,4},{4,5},{5,6},{6,7},{7,8},{8,9},{9,10},{10,1... | collective-permute-start | bytes 393224 | tf_op jit(solution)/shard_map/ppermute | solution.py:35
  87.2 5.9 %collective-permute-start.14 = (f32[2,1,128,128]{3,2,1,0:T(8,128)S(1)}, f32[2,1,128,128]{3,2,1,0:T(8,128)S(1)}, u32[]{:S(2)}, u32[]{:S(2)}) collective-permute-start(f32[2,1,128,128]{3,2,1,0:T(8,128)S(1)} %get-tuple-element.52), channel_id=1, source_target_pairs={{0,1},{1,2},{2,3},{3,4},{4,5},{5,6},{6,7},{7,8},{8,9},{9,10},{10,1... | collective-permute-start | bytes 393224 | tf_op jit(solution)/shard_map/ppermute | solution.py:35
  91.8 5.2 %collective-permute-start.15 = (f32[2,1,128,128]{3,2,1,0:T(8,128)S(1)}, f32[2,1,128,128]{3,2,1,0:T(8,128)S(1)}, u32[]{:S(2)}, u32[]{:S(2)}) collective-permute-start(f32[2,1,128,128]{3,2,1,0:T(8,128)S(1)} %get-tuple-element.53), channel_id=1, source_target_pairs={{1,0},{2,1},{3,2},{4,3},{5,4},{6,5},{7,6},{8,7},{9,8},{10,9},{11,1... | collective-permute-start | bytes 393224 | tf_op jit(solution)/shard_map/ppermute | solution.py:37
  102.0 7.4 %collective-permute-start.16 = (f32[2,1,128,128]{3,2,1,0:T(8,128)}, f32[2,1,128,128]{3,2,1,0:T(8,128)S(1)}, u32[]{:S(2)}, u32[]{:S(2)}) collective-permute-start(f32[2,1,128,128]{3,2,1,0:T(8,128)} %get-tuple-element.50), channel_id=1, source_target_pairs={{1,0},{2,1},{3,2},{4,3},{5,4},{6,5},{7,6},{8,7},{9,8},{10,9},{11,1... | collective-permute-start | bytes 393224 | tf_op jit(solution)/shard_map/ppermute | solution.py:37
  103.3 7.3 %collective-permute-start.17 = (f32[2,1,128,128]{3,2,1,0:T(8,128)}, f32[2,1,128,128]{3,2,1,0:T(8,128)S(1)}, u32[]{:S(2)}, u32[]{:S(2)}) collective-permute-start(f32[2,1,128,128]{3,2,1,0:T(8,128)} %get-tuple-element.51), channel_id=1, source_target_pairs={{0,1},{1,2},{2,3},{3,4},{4,5},{5,6},{6,7},{7,8},{8,9},{9,10},{10,1... | collective-permute-start | bytes 393224 | tf_op jit(solution)/shard_map/ppermute | solution.py:35
  116.8 9.4 %collective-permute-start.18 = (f32[2,1,128,128]{3,2,1,0:T(8,128)S(1)}, f32[2,1,128,128]{3,2,1,0:T(8,128)S(1)}, u32[]{:S(2)}, u32[]{:S(2)}) collective-permute-start(f32[2,1,128,128]{3,2,1,0:T(8,128)S(1)} %get-tuple-element.48), channel_id=1, source_target_pairs={{0,1},{1,2},{2,3},{3,4},{4,5},{5,6},{6,7},{7,8},{8,9},{9,10},{10,1... | collective-permute-start | bytes 393224 | tf_op jit(solution)/shard_map/ppermute | solution.py:35
  123.4 7.3 %collective-permute-start.19 = (f32[2,1,128,128]{3,2,1,0:T(8,128)S(1)}, f32[2,1,128,128]{3,2,1,0:T(8,128)}, u32[]{:S(2)}, u32[]{:S(2)}) collective-permute-start(f32[2,1,128,128]{3,2,1,0:T(8,128)S(1)} %get-tuple-element.49), channel_id=1, source_target_pairs={{1,0},{2,1},{3,2},{4,3},{5,4},{6,5},{7,6},{8,7},{9,8},{10,9},{11,1... | collective-permute-start | bytes 393224 | tf_op jit(solution)/shard_map/ppermute | solution.py:37
  136.9 10.5 %collective-permute-start.20 = (f32[2,1,128,128]{3,2,1,0:T(8,128)}, f32[2,1,128,128]{3,2,1,0:T(8,128)S(1)}, u32[]{:S(2)}, u32[]{:S(2)}) collective-permute-start(f32[2,1,128,128]{3,2,1,0:T(8,128)} %get-tuple-element.46), channel_id=1, source_target_pairs={{1,0},{2,1},{3,2},{4,3},{5,4},{6,5},{7,6},{8,7},{9,8},{10,9},{11,1... | collective-permute-start | bytes 393224 | tf_op jit(solution)/shard_map/ppermute | solution.py:37
  138.2 9.4 %collective-permute-start.21 = (f32[2,1,128,128]{3,2,1,0:T(8,128)}, f32[2,1,128,128]{3,2,1,0:T(8,128)S(1)}, u32[]{:S(2)}, u32[]{:S(2)}) collective-permute-start(f32[2,1,128,128]{3,2,1,0:T(8,128)} %get-tuple-element.47), channel_id=1, source_target_pairs={{0,1},{1,2},{2,3},{3,4},{4,5},{5,6},{6,7},{7,8},{8,9},{9,10},{10,1... | collective-permute-start | bytes 393224 | tf_op jit(solution)/shard_map/ppermute | solution.py:35
  153.0 7.9 %collective-permute-start.22 = (f32[2,1,128,128]{3,2,1,0:T(8,128)S(1)}, f32[2,1,128,128]{3,2,1,0:T(8,128)S(1)}, u32[]{:S(2)}, u32[]{:S(2)}) collective-permute-start(f32[2,1,128,128]{3,2,1,0:T(8,128)S(1)} %get-tuple-element.44), channel_id=1, source_target_pairs={{0,1},{1,2},{2,3},{3,4},{4,5},{5,6},{6,7},{7,8},{8,9},{9,10},{10,1... | collective-permute-start | bytes 393224 | tf_op jit(solution)/shard_map/ppermute | solution.py:35
  159.6 7.4 %collective-permute-start.23 = (f32[2,1,128,128]{3,2,1,0:T(8,128)S(1)}, f32[2,1,128,128]{3,2,1,0:T(8,128)S(1)}, u32[]{:S(2)}, u32[]{:S(2)}) collective-permute-start(f32[2,1,128,128]{3,2,1,0:T(8,128)S(1)} %get-tuple-element.45), channel_id=1, source_target_pairs={{1,0},{2,1},{3,2},{4,3},{5,4},{6,5},{7,6},{8,7},{9,8},{10,9},{11,1... | collective-permute-start | bytes 393224 | tf_op jit(solution)/shard_map/ppermute | solution.py:37
  210.2 11.2 %collective-permute-start.24 = (f32[2,512]{0,1:T(8,128)S(1)}, f32[2,512]{0,1:T(8,128)S(1)}, u32[]{:S(2)}, u32[]{:S(2)}) collective-permute-start(f32[2,512]{0,1:T(8,128)S(1)} %bitcast.98), channel_id=1, source_target_pairs={{0,1},{1,0},{2,3},{3,2},{4,5},{5,4},{6,7},{7,6},{8,9},{9,8},{10,11... | collective-permute-start | bytes 12296 | tf_op jit(solution)/shard_map/ppermute | solution.py:20
  217.0 53.2 %all-to-all-start = ((f32[2,4,128,128]{3,1,0,2:T(4,128)}), f32[2,4,128,128]{3,1,0,2:T(4,128)S(1)}, u32[]{:S(2)}, u32[]{:S(2)}) async-start(f32[2,4,128,128]{3,1,0,2:T(4,128)} %copy.32), calls=%async_computation | async-start | bytes 1048576 | tf_op jit(solution)/shard_map/all_to_all | solution.py:155
  221.4 15.5 %collective-permute-start.25 = (f32[2,512]{0,1:T(8,128)S(1)}, f32[2,512]{0,1:T(8,128)S(1)}, u32[]{:S(2)}, u32[]{:S(2)}) collective-permute-start(f32[2,512]{0,1:T(8,128)S(1)} %bitcast_add_fusion), channel_id=1, source_target_pairs={{0,2},{1,3},{2,0},{3,1},{4,6},{5,7},{6,4},{7,5},{8,10},{9,11},{10,... | collective-permute-start | bytes 12296 | tf_op jit(solution)/shard_map/ppermute | solution.py:20
  237.0 23.3 %collective-permute-start.26 = (f32[2,512]{0,1:T(8,128)S(1)}, f32[2,512]{0,1:T(8,128)S(1)}, u32[]{:S(2)}, u32[]{:S(2)}) collective-permute-start(f32[2,512]{0,1:T(8,128)S(1)} %add.1001), channel_id=1, source_target_pairs={{0,4},{1,5},{2,6},{3,7},{4,0},{5,1},{6,2},{7,3},{8,12},{9,13},{10,... | collective-permute-start | bytes 12296 | tf_op jit(solution)/shard_map/ppermute | solution.py:20
  260.3 6.9 %collective-permute-start.27 = (f32[2,512]{0,1:T(8,128)S(1)}, f32[2,512]{0,1:T(8,128)S(1)}, u32[]{:S(2)}, u32[]{:S(2)}) collective-permute-start(f32[2,512]{0,1:T(8,128)S(1)} %add.1002), channel_id=1, source_target_pairs={{0,8},{1,9},{2,10},{3,11},{4,12},{5,13},{6,14},{7,15},{8,0},{9,1},... | collective-permute-start | bytes 12296 | tf_op jit(solution)/shard_map/ppermute | solution.py:20
  267.2 8.0 %collective-permute-start.28 = (f32[2,512]{0,1:T(8,128)S(1)}, f32[2,512]{0,1:T(8,128)S(1)}, u32[]{:S(2)}, u32[]{:S(2)}) collective-permute-start(f32[2,512]{0,1:T(8,128)S(1)} %add.1003), channel_id=1, source_target_pairs={{0,16},{1,17},{2,18},{3,19},{4,20},{5,21},{6,22},{7,23},{8,24},{9,... | collective-permute-start | bytes 12296 | tf_op jit(solution)/shard_map/ppermute | solution.py:20
  356.4 63.8 %copy-start.20 = (f32[8,512]{1,0:T(8,128)S(1)}, f32[8,512]{1,0:T(8,128)}, u32[]{:S(2)}) copy-start(f32[8,512]{1,0:T(8,128)} %param.19) | copy-start | bytes 49156
  356.4 63.8 %copy-start.22 = (f32[512]{0:T(512)S(1)}, f32[512]{0:T(512)}, u32[]{:S(2)}) copy-start(f32[512]{0:T(512)} %param.17) | copy-start | bytes 6148
  (22 other events, 225.4 us)
